TPU v7x, 1024 devices: a whole 8x8x8 slice. The times are simulated.
1024 devices in a mesh: row: 64 (over x, y), col: 16 (over z, core).
Axes of the slice: x: 8, y: 8, z: 8, core: 2. Of those that a mesh axis runs over, the one named last changes fastest.
Arguments:
- matrix: float32 [32768, 8192], P('row', 'col'), may hold values from -50 to 50, as said below
Outputs:
- updated: float32 [32768, 8192], P('row', 'col')
- coefficients: float32 [512, 8192], P(None, 'col')
Inputs may be any that keep to these rules, and one draw needn't show every extreme that they name: `matrix`: real values of order one to some tens.
All inputs are finite; a program needn't handle non-finite values.
Results may differ from a plain program's by a relative error of at most 0.00014.
Values sent between devices are 32-bit elements; how exact they have to be, the bound alone decides.
A program may use at most 64 MiB of HBM per device.

v0:
```python
import functools
import math

import jax
import jax.numpy as jnp
from jax import lax
from jax.experimental import pallas as pl
from jax.experimental.pallas import tpu as pltpu
from jax.sharding import PartitionSpec as P

PANEL = 256
N = 8
CH = 8
CR = PANEL // CH
PIECE = 64
SUBS = ((0, 40), (40, 32))
MESH = pl.DeviceIdType.MESH
HI = lax.Precision.HIGHEST
F32 = jnp.float32


def wrap(i):
    return lax.rem(i + 2 * N, N)


def tdot(a, b, precision=HI):
    return lax.dot_general(a, b, (((0,), (0,)), ((), ())), precision=precision, preferred_element_type=F32)


def dot(a, b, precision=HI):
    return lax.dot_general(a, b, (((1,), (0,)), ((), ())), precision=precision, preferred_element_type=F32)


def dott(a, b, precision=HI):
    return lax.dot_general(a, b, (((1,), (1,)), ((), ())), precision=precision, preferred_element_type=F32)


def reduce_kernel(
    x_ref, p_ref, cf, gall,
    own, rf, rb, stage, r2, gtmp,
    zs, zr, cs, cr,
    fs, fr, bs, br,
    s2, q2, s3, q3, sg, qg,
    afs, afr, abs_, abr,
    gfs, gfr, gbs, gbr, gcs, gcr,
):
    row, col = lax.axis_index("row"), lax.axis_index("col")
    xx, yy = row // N, lax.rem(row, N)
    zz, cc = col // 2, lax.rem(col, 2)
    fwd = 1 - 2 * cc
    main, other = (xx, yy), (yy, xx)

    def at_main(k, m):
        return (m * N + yy, col) if k == 0 else (xx * N + m, col)

    def at_other(k, o):
        return at_main(1 - k, o)

    def at_z(z):
        return (row, wrap(z) * 2 + cc)

    mate = (row, zz * 2 + 1 - cc)

    def remote(src, dst, send, recv, device):
        return pltpu.make_async_remote_copy(
            src_ref=src, dst_ref=dst, send_sem=send, recv_sem=recv, device_id=device, device_id_type=MESH
        )

    barrier = pltpu.get_barrier_semaphore()
    partners = [at_main(k, wrap(main[k] + o)) for k in range(2) for o in range(1, N)]
    partners += [at_z(zz + 1), at_z(zz - 1), mate]
    for device in partners:
        pl.semaphore_signal(barrier, inc=1, device_id=device, device_id_type=MESH)
    pl.semaphore_wait(barrier, len(partners))

    def chunk(h, i):
        return pl.ds(pl.multiple_of(h * PANEL + i * CR, CR), CR)

    def z_copy(h, i, src):
        target = p_ref.at[cc, chunk(h, i), :]
        return remote(src, target, zs.at[h, i], zr.at[h, i], at_z(zz + 1 - 2 * h))

    def mate_copy(h, i, src):
        target = p_ref.at[cc, chunk(h, i), :]
        return remote(src, target, cs.at[h, i], cr.at[h, i], mate)

    @pl.when(zz == 0)
    def _():
        @pl.loop(0, CH)
        def _(i):
            for h in range(2):
                z_copy(h, i, x_ref.at[chunk(h, i), pl.ds(0, PANEL)]).start()
            for h in range(2):
                mate_copy(h, i, x_ref.at[chunk(h, i), pl.ds(0, PANEL)]).start()

        p_ref[cc] = x_ref[:, :PANEL]

    @pl.when(zz != 0)
    def _():
        @pl.loop(0, CH)
        def _(i):
            for h in range(2):
                here = p_ref.at[cc, chunk(h, i), :]
                z_copy(h, i, here).wait_recv()

                @pl.when(zz != (N - 1 if h == 0 else 1))
                def _():
                    z_copy(h, i, here).start()

                mate_copy(h, i, here).start()

    @pl.loop(0, CH)
    def _(i):
        for h in range(2):
            pltpu.make_async_remote_copy(
                src_ref=p_ref.at[1 - cc, chunk(h, i), :],
                dst_ref=p_ref.at[1 - cc, chunk(h, i), :],
                send_sem=cs.at[h, i],
                recv_sem=cr.at[h, i],
                device_id=mate,
                device_id_type=MESH,
            ).wait_recv()

    x = x_ref[...]

    @pl.loop(0, 4)
    def _(b):
        block = p_ref[b // 2, :, pl.ds(pl.multiple_of(128 * lax.rem(b, 2), 128), 128)]
        terms = tdot(block, x)
        for k in range(2):
            for j in range(2):
                own[k, 2 * b + j, 0:PIECE, :] = terms[PIECE * j : PIECE * (j + 1), PANEL * k : PANEL * (k + 1)]

    gb = col // 4
    block = p_ref[gb // 2, :, pl.ds(pl.multiple_of(128 * lax.rem(gb, 2), 128), 128)]
    for k in range(2):
        gtmp[k] = tdot(block, p_ref[k])
    for k in range(2):
        for j in range(N):
            first = pl.multiple_of(32 * lax.rem(col, 4) + 8 * (j // 2), 8)
            own[k, j, PIECE : PIECE + 8, 0:128] = gtmp[k, pl.ds(first, 8), 128 * (j % 2) : 128 * (j % 2) + 128]
            own[k, j, PIECE : PIECE + 8, 128:PANEL] = jnp.zeros((8, PANEL - 128), F32)

    def f_copy(k, s, u):
        rows = pl.ds(*SUBS[u])
        src = own.at[k, wrap(main[k] + 4 * fwd), rows, :] if s == 0 else rf.at[k, s - 1, rows, :]
        return remote(src, rf.at[k, s, rows, :], fs.at[k, s, u], fr.at[k, s, u], at_main(k, wrap(main[k] + fwd)))

    def b_copy(k, s, u):
        rows = pl.ds(*SUBS[u])
        src = own.at[k, wrap(main[k] - 3 * fwd), rows, :] if s == 0 else rb.at[k, s - 1, rows, :]
        return remote(src, rb.at[k, s, rows, :], bs.at[k, s, u], br.at[k, s, u], at_main(k, wrap(main[k] - fwd)))

    for u in range(2):
        for k in range(2):
            f_copy(k, 0, u).start()
            b_copy(k, 0, u).start()
    for s in range(1, 4):
        for u in range(2):
            rows = pl.ds(*SUBS[u])
            for k in range(2):
                f_copy(k, s - 1, u).wait_recv()
                rf[k, s - 1, rows, :] += own[k, wrap(main[k] + (4 - s) * fwd), rows, :]
                f_copy(k, s, u).start()
                if s < 3:
                    b_copy(k, s - 1, u).wait_recv()
                    rb[k, s - 1, rows, :] += own[k, wrap(main[k] - (3 - s) * fwd), rows, :]
                    b_copy(k, s, u).start()
    for k in range(2):
        for u in range(2):
            b_copy(k, 2, u).wait_recv()
            f_copy(k, 3, u).wait_recv()
        total = own[k, main[k]] + rf[k, 3] + rb[k, 2]
        for i in range(N):
            stage[k, i, 0:8, :] = total[8 * i : 8 * i + 8, :]
            stage[k, i, 8:16, :] = total[PIECE : PIECE + 8, :]
        for o in range(1, N):
            peer = wrap(other[k] + o)
            remote(stage.at[k, peer], r2.at[k, other[k]], s2.at[k, o - 1], q2.at[k, other[k]], at_other(k, peer)).start()
        r2[k, other[k]] = stage[k, other[k]]

    def mine(k):
        return pl.ds(pl.multiple_of(PIECE * main[k] + 8 * other[k], 8), 8)

    for k in range(2):
        for o in range(1, N):
            peer = wrap(other[k] + o)
            remote(stage.at[k, peer], r2.at[k, peer], s2.at[k, o - 1], q2.at[k, peer], at_other(k, peer)).wait_recv()
        total = r2[k, 0]
        for o in range(1, N):
            total = total + r2[k, o]
        cf[k, mine(k), :] = total[0:8, :]
        gall[col, k, main[k]] = total[8:16, 0:128]
        for o in range(1, N):
            peer = wrap(main[k] + o)
            tile = gall.at[col, k, main[k]]
            remote(tile, tile, sg.at[k, o - 1], qg.at[k, main[k]], at_main(k, peer)).start()
        for o in range(1, N):
            peer = wrap(other[k] + o)
            rows = cf.at[k, mine(k), :]
            remote(rows, rows, s3.at[k, o - 1], q3.at[k, other[k]], at_other(k, peer)).start()

    def gf_copy(s):
        slab = gall.at[wrap(zz - s * fwd) * 2 + cc]
        return remote(slab, slab, gfs.at[s], gfr.at[s], at_z(zz + fwd))

    def gb_copy(s):
        slab = gall.at[wrap(zz + s * fwd) * 2 + cc]
        return remote(slab, slab, gbs.at[s], gbr.at[s], at_z(zz - fwd))

    def gf_wait(s):
        slab = gall.at[wrap(zz - (s + 1) * fwd) * 2 + cc]
        remote(slab, slab, gfs.at[s], gfr.at[s], at_z(zz + fwd)).wait_recv()

    def gb_wait(s):
        slab = gall.at[wrap(zz + (s + 1) * fwd) * 2 + cc]
        remote(slab, slab, gbs.at[s], gbr.at[s], at_z(zz - fwd)).wait_recv()

    def g_mate(z):
        slab = gall.at[z * 2 + cc]
        return remote(slab, slab, gcs.at[z], gcr.at[z], mate)

    for k in range(2):
        for o in range(1, N):
            peer = wrap(main[k] + o)
            tile = gall.at[col, k, peer]
            remote(tile, tile, sg.at[k, o - 1], qg.at[k, peer], at_main(k, peer)).wait_recv()
    gf_copy(0).start()
    gb_copy(0).start()
    g_mate(zz).start()

    def piece(k, m, u):
        return cf.at[k, pl.ds(pl.multiple_of(PIECE * wrap(m) + 32 * u, 32), 32), :]

    def af_copy(k, s, u, m):
        return remote(piece(k, m, u), piece(k, m, u), afs.at[k, s, u], afr.at[k, s, u], at_main(k, wrap(main[k] + fwd)))

    def ab_copy(k, s, u, m):
        return remote(piece(k, m, u), piece(k, m, u), abs_.at[k, s, u], abr.at[k, s, u], at_main(k, wrap(main[k] - fwd)))

    for k in range(2):
        for o in range(1, N):
            peer = wrap(other[k] + o)
            rows = cf.at[k, pl.ds(pl.multiple_of(PIECE * main[k] + 8 * peer, 8), 8), :]
            remote(rows, rows, s3.at[k, o - 1], q3.at[k, peer], at_other(k, peer)).wait_recv()
        for u in range(2):
            af_copy(k, 0, u, main[k]).start()
            ab_copy(k, 0, u, main[k]).start()
    for s in range(1, 5):
        for u in range(2):
            for k in range(2):
                af_copy(k, s - 1, u, main[k] - s * fwd).wait_recv()
                if s < 4:
                    af_copy(k, s, u, main[k] - s * fwd).start()
                    ab_copy(k, s - 1, u, main[k] + s * fwd).wait_recv()
                if s < 3:
                    ab_copy(k, s, u, main[k] + s * fwd).start()
        gf_wait(s - 1)
        if s < 4:
            gf_copy(s).start()
        g_mate(wrap(zz - s * fwd)).start()
        if s < 4:
            gb_wait(s - 1)
            if s < 3:
                gb_copy(s).start()
            g_mate(wrap(zz + s * fwd)).start()
    for z in range(N):
        slab = gall.at[z * 2 + 1 - cc]
        remote(slab, slab, gcs.at[z], gcr.at[z], mate).wait_recv()

    @pl.loop(0, CH)
    def _(i):
        for h in range(2):
            here = p_ref.at[cc, chunk(h, i), :]
            mate_copy(h, i, here).wait_send()

            @pl.when(zz != (N - 1 if h == 0 else 1))
            def _():
                z_copy(h, i, here).wait_send()

    for k in range(2):
        for u in range(2):
            for s in range(4):
                f_copy(k, s, u).wait_send()
                af_copy(k, s, u, main[k]).wait_send()
            for s in range(3):
                b_copy(k, s, u).wait_send()
                ab_copy(k, s, u, main[k]).wait_send()
        for o in range(1, N):
            peer = wrap(other[k] + o)
            remote(stage.at[k, peer], r2.at[k, peer], s2.at[k, o - 1], q2.at[k, peer], at_other(k, peer)).wait_send()
            rows = cf.at[k, mine(k), :]
            remote(rows, rows, s3.at[k, o - 1], q3.at[k, peer], at_other(k, peer)).wait_send()
            tile = gall.at[col, k, main[k]]
            remote(tile, tile, sg.at[k, o - 1], qg.at[k, peer], at_main(k, wrap(main[k] + o))).wait_send()
    for s in range(4):
        gf_copy(s).wait_send()
    for s in range(3):
        gb_copy(s).wait_send()
    for z in range(N):
        g_mate(z).wait_send()


def reduced(matrix):
    dma = pltpu.SemaphoreType.DMA
    out = lambda *shape: jax.ShapeDtypeStruct(shape, F32)
    vmem = pl.BlockSpec(memory_space=pltpu.VMEM)
    return pl.pallas_call(
        reduce_kernel,
        out_shape=(out(2, 512, PANEL), out(2, 512, PANEL), out(16, 2, N, 8, 128)),
        in_specs=[vmem],
        out_specs=(vmem, vmem, vmem),
        scratch_shapes=[
            pltpu.VMEM((2, N, 72, PANEL), F32),
            pltpu.VMEM((2, 4, 72, PANEL), F32),
            pltpu.VMEM((2, 3, 72, PANEL), F32),
            pltpu.VMEM((2, N, 16, PANEL), F32),
            pltpu.VMEM((2, N, 16, PANEL), F32),
            pltpu.VMEM((2, 128, PANEL), F32),
            dma((2, CH)), dma((2, CH)), dma((2, CH)), dma((2, CH)),
            dma((2, 4, 2)), dma((2, 4, 2)), dma((2, 3, 2)), dma((2, 3, 2)),
            dma((2, N - 1)), dma((2, N)), dma((2, N - 1)), dma((2, N)), dma((2, N - 1)), dma((2, N)),
            dma((2, 4, 2)), dma((2, 4, 2)), dma((2, 3, 2)), dma((2, 3, 2)),
            dma((4,)), dma((4,)), dma((3,)), dma((3,)), dma((N,)), dma((N,)),
        ],
        compiler_params=pltpu.CompilerParams(collective_id=0, has_side_effects=True),
    )(matrix)


def solve_kernel(stretch, x_ref, p_ref, cf, gall, upd, w_ref, g, m, t, e, bt, dcol, drow):
    n = 2 * PANEL
    col = lax.axis_index("col")

    @pl.loop(0, 16)
    def _(c):
        for k in range(2):
            for j in range(N):
                rows = pl.ds(pl.multiple_of(32 * c + 8 * (j // 2), 8), 8)
                g[rows, PANEL * k + 128 * (j % 2) : PANEL * k + 128 * (j % 2) + 128] = gall[c, k, j]

    i_row = lax.broadcasted_iota(jnp.int32, (n, n), 0)
    i_col = lax.broadcasted_iota(jnp.int32, (n, n), 1)
    eye = i_row == i_col
    diagonal = jnp.where(eye, g[...], 0.0)
    dcol[...] = lax.rsqrt(jnp.sum(diagonal, axis=1, keepdims=True))
    drow[...] = lax.rsqrt(jnp.sum(diagonal, axis=0, keepdims=True))
    g[...] = g[...] * dcol[...] * drow[...]

    def half_lower(v):
        return jnp.where(i_row > i_col, v, jnp.where(eye, 0.5 * v, 0.0))

    ident = jnp.where(eye, 1.0, 0.0)
    m[...] = ident - half_lower(g[...] - ident)

    halves = [pl.ds(0, PANEL), pl.ds(PANEL, PANEL)]

    def refine(precision):
        for h in halves:
            t[:, h] = dot(m[...], g[:, h], precision)
        for h in halves:
            e[:, h] = dott(t[...], m[h, :], precision)
        e[...] = e[...] - ident
        square = jnp.sum(e[...] * e[...])
        e[...] = half_lower(e[...])
        for h in halves:
            t[:, h] = m[:, h] - dot(e[...], m[:, h], precision)
        m[...] = t[...]
        return square

    refine(HI)
    refine(HI)
    left = refine(HI)

    @pl.when(jnp.logical_not(left < 1e-6))
    def _():
        t[...] = ident

        @pl.loop(0, n)
        def _(j):
            g_row = g[pl.ds(j, 1), :]
            t_row = t[pl.ds(j, 1), :]
            lane = lax.broadcasted_iota(jnp.int32, (n, n), 1)
            column = jnp.sum(jnp.where(lane == j, g[...], 0.0), axis=1, keepdims=True)
            one_lane = lax.broadcasted_iota(jnp.int32, (1, n), 1)
            pivot = jnp.sum(jnp.where(one_lane == j, g_row, 0.0), axis=1, keepdims=True)
            down = lax.broadcasted_iota(jnp.int32, (n, 1), 0)
            factor = jnp.where(down > j, column / pivot, 0.0)
            scale = jnp.where(down == j, lax.rsqrt(pivot), 1.0)
            g[...] = g[...] - factor * g_row
            t[...] = (t[...] - factor * t_row) * scale

        m[...] = t[...]

    m[...] = m[...] * drow[...]
    top, low = halves
    w_top = w_ref.at[top, :]
    for k, h in enumerate(halves):
        c_top, c_low = cf[k, top, :], cf[k, low, :]
        w_ref[top, h] = dot(m[top, top], c_top)
        w_ref[low, h] = dot(m[low, top], c_top) + dot(m[low, low], c_low)
    bt[:, top] = dott(p_ref[0], m[top, top])
    bt[:, low] = dott(p_ref[0], m[low, top]) + dott(p_ref[1], m[low, low])
    upd[:, low] = x_ref[:, low] - dot(bt[...], w_ref[:, low])
    first = x_ref[:, top] - dot(bt[:, top], w_ref[top, top])
    first = jnp.where(col == 0, stretch * bt[:, top], first)
    first = first - dot(bt[:, low], w_ref[low, top])
    upd[:, top] = jnp.where(col == 1, stretch * bt[:, low], first)


def solved(stretch, matrix, panels, cross, gram):
    vmem = pl.BlockSpec(memory_space=pltpu.VMEM)
    square = pltpu.VMEM((512, 512), F32)
    return pl.pallas_call(
        functools.partial(solve_kernel, stretch),
        out_shape=(jax.ShapeDtypeStruct((512, 512), F32), jax.ShapeDtypeStruct((512, 512), F32)),
        in_specs=[vmem] * 4,
        out_specs=(vmem, vmem),
        scratch_shapes=[square] * 5 + [pltpu.VMEM((512, 1), F32), pltpu.VMEM((1, 512), F32)],
    )(matrix, panels, cross, gram)


def body(matrix):
    stretch = math.sqrt(lax.axis_size("row") * matrix.shape[0])
    panels, cross, gram = reduced(matrix)
    return solved(stretch, matrix, panels, cross, gram)


def solution(mesh):
    in_specs = (P("row", "col"),)
    out_specs = (P("row", "col"), P(None, "col"))
    return jax.shard_map(body, mesh=mesh, in_specs=in_specs, out_specs=out_specs, check_vma=False)
```

profile of v0, /device:TPU:1, one launch (start us, length us, event | category | flops | bytes accessed | tf_op | source)
XLA Modules:
  0.0 579.1 jit_solution(13951235411675287317)
XLA Ops:
  0.6 362.0 %shard_map.30 = (f32[2,512,256]{2,1,0:T(8,128)}, f32[2,512,256]{2,1,0:T(8,128)}, f32[16,2,8,8,128]{4,3,2,1,0:T(8,128)}) custom-call(f32[512,512]{1,0:T(8,128)} %x_ref.3), custom_call_target="tpu_custom_call" | custom-call | tf_op jit(solution)/shard_map/pallas_call | solution.py:308
  362.6 216.4 %shard_map.31 = (f32[512,512]{1,0:T(8,128)}, f32[512,512]{1,0:T(8,128)}) custom-call(f32[512,512]{1,0:T(8,128)} %x_ref.3, f32[2,512,256]{2,1,0:T(8,128)} %get-tuple-element.5.p_ref, f32[2,512,256]{2,1,0:T(8,128)} %get-tuple-element.6.cf, f32[16,2,8,8,128]{4,3,2,1,0:T(8,128)} %get-tuple-element.7.gall), custom_call_target="tpu_custom_call" | custom-call | tf_op jit(solution)/shard_map/pallas_call | solution.py:413
where the time goes:
time: 579 us
  Pallas kernels  578 us (100%)
    pallas_call x1, Pallas kernels, reduced(): pl.pallas_call(reduce_kernel, out_shape=(out(2, 512, PANEL), out(2, 512,...  362 us
    pallas_call x1, Pallas kernels, solved(): pl.pallas_call(functools.partial(solve_kernel, stretch), out_shape=(jax.S...  216 us

commit v1 on v0

v1 whole, which is shorter than its diff:
```python
import functools
import math

import jax
import jax.numpy as jnp
from jax import lax
from jax.experimental import pallas as pl
from jax.experimental.pallas import tpu as pltpu
from jax.sharding import PartitionSpec as P

PANEL = 256
N = 8
CH = 16
CR = 512 // CH
PIECE = 64
PEERS = (1, N - 1, 2, N - 2, 3, N - 3, 4)
MESH = pl.DeviceIdType.MESH
HI = lax.Precision.HIGHEST
F32 = jnp.float32


def wrap(i):
    return lax.rem(i + 2 * N, N)


def tdot(a, b, precision=HI):
    return lax.dot_general(a, b, (((0,), (0,)), ((), ())), precision=precision, preferred_element_type=F32)


def dot(a, b, precision=HI):
    return lax.dot_general(a, b, (((1,), (0,)), ((), ())), precision=precision, preferred_element_type=F32)


def dott(a, b, precision=HI):
    return lax.dot_general(a, b, (((1,), (1,)), ((), ())), precision=precision, preferred_element_type=F32)


def reduce_kernel(
    x_ref, p_ref, cf, gall,
    own, r1, stage, r2, gtmp,
    zs, zr, cs, cr,
    s1, q1, s2, q2, s3, q3, s4, q4,
    sg, qg, sz, qz, sc, qc,
):
    row, col = lax.axis_index("row"), lax.axis_index("col")
    xx, yy = row // N, lax.rem(row, N)
    zz, cc = col // 2, lax.rem(col, 2)
    step = 1 - 2 * (zz // 5)
    main, other = (xx, yy), (yy, xx)

    def at_main(k, m):
        return (m * N + yy, col) if k == 0 else (xx * N + m, col)

    def at_other(k, o):
        return at_main(1 - k, o)

    def at_z(z):
        return (row, wrap(z) * 2 + cc)

    mate = (row, zz * 2 + 1 - cc)

    def remote(src, dst, send, recv, device):
        return pltpu.make_async_remote_copy(
            src_ref=src, dst_ref=dst, send_sem=send, recv_sem=recv, device_id=device, device_id_type=MESH
        )

    barrier = pltpu.get_barrier_semaphore()
    partners = [at_main(k, wrap(main[k] + o)) for k in range(2) for o in range(1, N)]
    partners += [at_z(zz + o) for o in range(1, N)] + [mate]
    for device in partners:
        pl.semaphore_signal(barrier, inc=1, device_id=device, device_id_type=MESH)
    pl.semaphore_wait(barrier, len(partners))

    def chunk(i):
        return pl.ds(pl.multiple_of(i * CR, CR), CR)

    def z_copy(h, i, src, z):
        return remote(src, p_ref.at[cc, chunk(i), :], zs.at[h, i], zr.at[i], at_z(z))

    def mate_copy(i, src):
        return remote(src, p_ref.at[cc, chunk(i), :], cs.at[i], cr.at[i], mate)

    @pl.when(zz == 0)
    def _():
        @pl.loop(0, CH)
        def _(i):
            here = x_ref.at[chunk(i), pl.ds(0, PANEL)]
            z_copy(0, i, here, 1).start()
            z_copy(1, i, here, N - 1).start()
            mate_copy(i, here).start()

        p_ref[cc] = x_ref[:, :PANEL]

    relays = (zz != 0) & (zz != 4) & (zz != 5)

    @pl.when(zz != 0)
    def _():
        @pl.loop(0, CH)
        def _(i):
            here = p_ref.at[cc, chunk(i), :]
            z_copy(0, i, here, zz + step).wait_recv()

            @pl.when(relays)
            def _():
                z_copy(0, i, here, zz + step).start()

            mate_copy(i, here).start()

    @pl.loop(0, CH)
    def _(i):
        here = p_ref.at[1 - cc, chunk(i), :]
        remote(here, here, cs.at[i], cr.at[i], mate).wait_recv()

    x = x_ref[...]

    @pl.loop(0, 4)
    def _(b):
        block = p_ref[b // 2, :, pl.ds(pl.multiple_of(128 * lax.rem(b, 2), 128), 128)]
        terms = tdot(block, x)
        for k in range(2):
            for j in range(2):
                own[k, 2 * b + j, 0:PIECE, :] = terms[PIECE * j : PIECE * (j + 1), PANEL * k : PANEL * (k + 1)]

    gb = col // 4
    block = p_ref[gb // 2, :, pl.ds(pl.multiple_of(128 * lax.rem(gb, 2), 128), 128)]
    for k in range(2):
        gtmp[k] = tdot(block, p_ref[k])
    for k in range(2):
        for j in range(N):
            first = pl.multiple_of(32 * lax.rem(col, 4) + 8 * (j // 2), 8)
            own[k, j, PIECE : PIECE + 8, 0:128] = gtmp[k, pl.ds(first, 8), 128 * (j % 2) : 128 * (j % 2) + 128]
            own[k, j, PIECE : PIECE + 8, 128:PANEL] = jnp.zeros((8, PANEL - 128), F32)

    def copy1(k, o, slot):
        peer = wrap(main[k] + o)
        return remote(own.at[k, peer], r1.at[k, slot], s1.at[k, o - 1], q1.at[k, slot], at_main(k, peer))

    def copy2(k, o, slot):
        peer = wrap(other[k] + o)
        return remote(stage.at[k, peer], r2.at[k, slot], s2.at[k, o - 1], q2.at[k, slot], at_other(k, peer))

    for o in PEERS:
        for k in range(2):
            copy1(k, o, main[k]).start()
    for k in range(2):
        r1[k, main[k]] = own[k, main[k]]
        for o in PEERS:
            copy1(k, o, wrap(main[k] + o)).wait_recv()
        total = r1[k, 0]
        for o in range(1, N):
            total = total + r1[k, o]
        for i in range(N):
            stage[k, i, 0:8, :] = total[8 * i : 8 * i + 8, :]
            stage[k, i, 8:16, :] = total[PIECE : PIECE + 8, :]
        for o in PEERS:
            copy2(k, o, other[k]).start()
        r2[k, other[k]] = stage[k, other[k]]

    def rows_of(k, i):
        return cf.at[k, pl.ds(pl.multiple_of(PIECE * main[k] + 8 * i, 8), 8), :]

    def piece_of(k, i):
        return cf.at[k, pl.ds(pl.multiple_of(PIECE * i, PIECE), PIECE), :]

    def copy3(k, o, i):
        return remote(rows_of(k, i), rows_of(k, i), s3.at[k, o - 1], q3.at[k, i], at_other(k, wrap(other[k] + o)))

    def copy4(k, o, i):
        return remote(piece_of(k, i), piece_of(k, i), s4.at[k, o - 1], q4.at[k, i], at_main(k, wrap(main[k] + o)))

    def tile_copy(k, o, i):
        tile = gall.at[col, k, i]
        return remote(tile, tile, sg.at[k, o - 1], qg.at[k, i], at_main(k, wrap(main[k] + o)))

    def slab_copy(o, z):
        slab = gall.at[z * 2 + cc]
        return remote(slab, slab, sz.at[o - 1], qz.at[z], at_z(zz + o))

    def slab_mate(z, core):
        slab = gall.at[z * 2 + core]
        return remote(slab, slab, sc.at[z], qc.at[z], mate)

    for k in range(2):
        for o in PEERS:
            copy2(k, o, wrap(other[k] + o)).wait_recv()
        total = r2[k, 0]
        for o in range(1, N):
            total = total + r2[k, o]
        gall[col, k, main[k]] = total[8:16, 0:128]
        cf[k, pl.ds(pl.multiple_of(PIECE * main[k] + 8 * other[k], 8), 8), :] = total[0:8, :]
        for o in PEERS:
            tile_copy(k, o, main[k]).start()
        for o in PEERS:
            copy3(k, o, other[k]).start()

    for k in range(2):
        for o in PEERS:
            tile_copy(k, o, wrap(main[k] + o)).wait_recv()
    for o in PEERS:
        slab_copy(o, zz).start()
    slab_mate(zz, cc).start()

    for k in range(2):
        for o in PEERS:
            copy3(k, o, wrap(other[k] + o)).wait_recv()
        for o in PEERS:
            copy4(k, o, main[k]).start()
    for o in PEERS:
        z = wrap(zz - o)
        slab_copy(o, z).wait_recv()
        slab_mate(z, cc).start()
    for k in range(2):
        for o in PEERS:
            copy4(k, o, wrap(main[k] + o)).wait_recv()
    for z in range(N):
        slab_mate(z, 1 - cc).wait_recv()

    @pl.loop(0, CH)
    def _(i):
        here = p_ref.at[cc, chunk(i), :]
        mate_copy(i, here).wait_send()

        @pl.when(relays | (zz == 0))
        def _():
            z_copy(0, i, here, zz + step).wait_send()

        @pl.when(zz == 0)
        def _():
            z_copy(1, i, here, N - 1).wait_send()

    for o in range(1, N):
        for k in range(2):
            copy1(k, o, main[k]).wait_send()
            copy2(k, o, other[k]).wait_send()
            copy3(k, o, other[k]).wait_send()
            copy4(k, o, main[k]).wait_send()
            tile_copy(k, o, main[k]).wait_send()
        slab_copy(o, zz).wait_send()
    for z in range(N):
        slab_mate(z, cc).wait_send()


def reduced(matrix):
    dma = pltpu.SemaphoreType.DMA
    out = lambda *shape: jax.ShapeDtypeStruct(shape, F32)
    vmem = pl.BlockSpec(memory_space=pltpu.VMEM)
    return pl.pallas_call(
        reduce_kernel,
        out_shape=(out(2, 512, PANEL), out(2, 512, PANEL), out(16, 2, N, 8, 128)),
        in_specs=[vmem],
        out_specs=(vmem, vmem, vmem),
        scratch_shapes=[
            pltpu.VMEM((2, N, 72, PANEL), F32),
            pltpu.VMEM((2, N, 72, PANEL), F32),
            pltpu.VMEM((2, N, 16, PANEL), F32),
            pltpu.VMEM((2, N, 16, PANEL), F32),
            pltpu.VMEM((2, 128, PANEL), F32),
            dma((2, CH)), dma((CH,)), dma((CH,)), dma((CH,)),
            *[dma((2, N))] * 8,
            dma((2, N)), dma((2, N)), dma((N,)), dma((N,)), dma((N,)), dma((N,)),
        ],
        compiler_params=pltpu.CompilerParams(collective_id=0, has_side_effects=True),
    )(matrix)


def solve_kernel(stretch, x_ref, p_ref, cf, gall, upd, w_ref, g, m, t, e, bt, dcol, drow):
    n = 2 * PANEL
    col = lax.axis_index("col")

    @pl.loop(0, 16)
    def _(c):
        for k in range(2):
            for j in range(N):
                rows = pl.ds(pl.multiple_of(32 * c + 8 * (j // 2), 8), 8)
                g[rows, PANEL * k + 128 * (j % 2) : PANEL * k + 128 * (j % 2) + 128] = gall[c, k, j]

    i_row = lax.broadcasted_iota(jnp.int32, (n, n), 0)
    i_col = lax.broadcasted_iota(jnp.int32, (n, n), 1)
    eye = i_row == i_col
    diagonal = jnp.where(eye, g[...], 0.0)
    dcol[...] = lax.rsqrt(jnp.sum(diagonal, axis=1, keepdims=True))
    drow[...] = lax.rsqrt(jnp.sum(diagonal, axis=0, keepdims=True))
    g[...] = g[...] * dcol[...] * drow[...]

    def half_lower(v):
        return jnp.where(i_row > i_col, v, jnp.where(eye, 0.5 * v, 0.0))

    ident = jnp.where(eye, 1.0, 0.0)
    m[...] = ident - half_lower(g[...] - ident)

    halves = [pl.ds(0, PANEL), pl.ds(PANEL, PANEL)]

    def refine(precision):
        for h in halves:
            t[:, h] = dot(m[...], g[:, h], precision)
        for h in halves:
            e[:, h] = dott(t[...], m[h, :], precision)
        e[...] = e[...] - ident
        square = jnp.sum(e[...] * e[...])
        e[...] = half_lower(e[...])
        for h in halves:
            t[:, h] = m[:, h] - dot(e[...], m[:, h], precision)
        m[...] = t[...]
        return square

    refine(HI)
    refine(HI)
    left = refine(HI)

    @pl.when(jnp.logical_not(left < 1e-6))
    def _():
        t[...] = ident

        @pl.loop(0, n)
        def _(j):
            g_row = g[pl.ds(j, 1), :]
            t_row = t[pl.ds(j, 1), :]
            lane = lax.broadcasted_iota(jnp.int32, (n, n), 1)
            column = jnp.sum(jnp.where(lane == j, g[...], 0.0), axis=1, keepdims=True)
            one_lane = lax.broadcasted_iota(jnp.int32, (1, n), 1)
            pivot = jnp.sum(jnp.where(one_lane == j, g_row, 0.0), axis=1, keepdims=True)
            down = lax.broadcasted_iota(jnp.int32, (n, 1), 0)
            factor = jnp.where(down > j, column / pivot, 0.0)
            scale = jnp.where(down == j, lax.rsqrt(pivot), 1.0)
            g[...] = g[...] - factor * g_row
            t[...] = (t[...] - factor * t_row) * scale

        m[...] = t[...]

    m[...] = m[...] * drow[...]
    top, low = halves
    for k, h in enumerate(halves):
        c_top, c_low = cf[k, top, :], cf[k, low, :]
        w_ref[top, h] = dot(m[top, top], c_top)
        w_ref[low, h] = dot(m[low, top], c_top) + dot(m[low, low], c_low)
    bt[:, top] = dott(p_ref[0], m[top, top])
    bt[:, low] = dott(p_ref[0], m[low, top]) + dott(p_ref[1], m[low, low])
    upd[:, low] = x_ref[:, low] - dot(bt[...], w_ref[:, low])
    first = x_ref[:, top] - dot(bt[:, top], w_ref[top, top])
    first = jnp.where(col == 0, stretch * bt[:, top], first)
    first = first - dot(bt[:, low], w_ref[low, top])
    upd[:, top] = jnp.where(col == 1, stretch * bt[:, low], first)


def solved(stretch, matrix, panels, cross, gram):
    vmem = pl.BlockSpec(memory_space=pltpu.VMEM)
    square = pltpu.VMEM((512, 512), F32)
    return pl.pallas_call(
        functools.partial(solve_kernel, stretch),
        out_shape=(jax.ShapeDtypeStruct((512, 512), F32), jax.ShapeDtypeStruct((512, 512), F32)),
        in_specs=[vmem] * 4,
        out_specs=(vmem, vmem),
        scratch_shapes=[square] * 5 + [pltpu.VMEM((512, 1), F32), pltpu.VMEM((1, 512), F32)],
    )(matrix, panels, cross, gram)


def body(matrix):
    stretch = math.sqrt(lax.axis_size("row") * matrix.shape[0])
    panels, cross, gram = reduced(matrix)
    return solved(stretch, matrix, panels, cross, gram)


def solution(mesh):
    in_specs = (P("row", "col"),)
    out_specs = (P("row", "col"), P(None, "col"))
    return jax.shard_map(body, mesh=mesh, in_specs=in_specs, out_specs=out_specs, check_vma=False)
```

time: 579 us -> 313 us (0.54)
  Pallas kernels: 578 us -> 313 us
    pallas_call x1, Pallas kernels: 362 us -> 96.1 us  [reduced(): pl.pallas_call(reduce_kernel, out_shape=(out(2, 512, PANEL), out(2, 512,...]
where the time goes in v1:
time: 313 us
  Pallas kernels  313 us (100%)
    pallas_call x1, Pallas kernels, solved(): pl.pallas_call(functools.partial(solve_kernel, stretch), out_shape=(jax.S...  216 us
    pallas_call x1, Pallas kernels, reduced(): pl.pallas_call(reduce_kernel, out_shape=(out(2, 512, PANEL), out(2, 512,...  96.1 us

profile of v1, /device:TPU:1, one launch (start us, length us, event | category | flops | bytes accessed | tf_op | source)
XLA Modules:
  0.0 313.2 jit_solution(5226514871327985442)
XLA Ops:
  0.6 96.1 %shard_map.30 = (f32[2,512,256]{2,1,0:T(8,128)}, f32[2,512,256]{2,1,0:T(8,128)}, f32[16,2,8,8,128]{4,3,2,1,0:T(8,128)}) custom-call(f32[512,512]{1,0:T(8,128)} %x_ref.3), custom_call_target="tpu_custom_call" | custom-call | tf_op jit(solution)/shard_map/pallas_call | solution.py:247
  96.7 216.4 %shard_map.31 = (f32[512,512]{1,0:T(8,128)}, f32[512,512]{1,0:T(8,128)}) custom-call(f32[512,512]{1,0:T(8,128)} %x_ref.3, f32[2,512,256]{2,1,0:T(8,128)} %get-tuple-element.5.p_ref, f32[2,512,256]{2,1,0:T(8,128)} %get-tuple-element.6.cf, f32[16,2,8,8,128]{4,3,2,1,0:T(8,128)} %get-tuple-element.7.gall), custom_call_target="tpu_custom_call" | custom-call | tf_op jit(solution)/shard_map/pallas_call | solution.py:348

commit v2 on v1

--- a/solution.py
+++ b/solution.py
@@ -282,29 +282,40 @@
     drow[...] = lax.rsqrt(jnp.sum(diagonal, axis=0, keepdims=True))
     g[...] = g[...] * dcol[...] * drow[...]
 
+    ident = jnp.where(eye, 1.0, 0.0)
+    b_row = lax.broadcasted_iota(jnp.int32, (PANEL, PANEL), 0)
+    b_col = lax.broadcasted_iota(jnp.int32, (PANEL, PANEL), 1)
+    b_eye = jnp.where(b_row == b_col, 1.0, 0.0)
+
     def half_lower(v):
-        return jnp.where(i_row > i_col, v, jnp.where(eye, 0.5 * v, 0.0))
-
-    ident = jnp.where(eye, 1.0, 0.0)
-    m[...] = ident - half_lower(g[...] - ident)
+        return jnp.where(b_row > b_col, v, 0.5 * b_eye * v)
 
     halves = [pl.ds(0, PANEL), pl.ds(PANEL, PANEL)]
+    top, low = halves
+    m[top, top] = b_eye - half_lower(g[top, top] - b_eye)
+    m[low, low] = b_eye - half_lower(g[low, low] - b_eye)
+    m[low, top] = -g[low, top]
+    m[top, low] = jnp.zeros((PANEL, PANEL), F32)
 
     def refine(precision):
+        t[top, top] = dot(m[top, top], g[top, top], precision)
         for h in halves:
-            t[:, h] = dot(m[...], g[:, h], precision)
-        for h in halves:
-            e[:, h] = dott(t[...], m[h, :], precision)
-        e[...] = e[...] - ident
-        square = jnp.sum(e[...] * e[...])
-        e[...] = half_lower(e[...])
-        for h in halves:
-            t[:, h] = m[:, h] - dot(e[...], m[:, h], precision)
-        m[...] = t[...]
+            t[low, h] = dot(m[low, top], g[top, h], precision) + dot(m[low, low], g[low, h], precision)
+        e00 = dott(t[top, top], m[top, top], precision) - b_eye
+        e10 = dott(t[low, top], m[top, top], precision)
+        e11 = dott(t[low, top], m[low, top], precision) + dott(t[low, low], m[low, low], precision) - b_eye
+        square = jnp.sum(e00 * e00 + 2.0 * e10 * e10 + e11 * e11)
+        e[top, top] = half_lower(e00)
+        e[low, top] = e10
+        e[low, low] = half_lower(e11)
+        below = dot(e[low, top], m[top, top], precision) + dot(e[low, low], m[low, top], precision)
+        m[low, top] = m[low, top] - below
+        m[top, top] = m[top, top] - dot(e[top, top], m[top, top], precision)
+        m[low, low] = m[low, low] - dot(e[low, low], m[low, low], precision)
         return square
 
-    refine(HI)
-    refine(HI)
+    refine(lax.Precision.DEFAULT)
+    refine(lax.Precision.HIGH)
     left = refine(HI)
 
     @pl.when(jnp.logical_not(left < 1e-6))
@@ -328,7 +339,6 @@
         m[...] = t[...]
 
     m[...] = m[...] * drow[...]
-    top, low = halves
     for k, h in enumerate(halves):
         c_top, c_low = cf[k, top, :], cf[k, low, :]
         w_ref[top, h] = dot(m[top, top], c_top)

time: 313 us -> 304 us (0.971)
  Pallas kernels: 313 us -> 303 us
    pallas_call x1, Pallas kernels: 216 us -> 207 us  [solved(): pl.pallas_call(functools.partial(solve_kernel, stretch), out_shape=(jax.S...]
where the time goes in v2:
time: 304 us
  Pallas kernels  303 us (100%)
    pallas_call x1, Pallas kernels, solved(): pl.pallas_call(functools.partial(solve_kernel, stretch), out_shape=(jax.S...  207 us
    pallas_call x1, Pallas kernels, reduced(): pl.pallas_call(reduce_kernel, out_shape=(out(2, 512, PANEL), out(2, 512,...  96.1 us

profile of v2, /device:TPU:1, one launch (start us, length us, event | category | flops | bytes accessed | tf_op | source)
XLA Modules:
  0.0 303.5 jit_solution(5485474389967795423)
XLA Ops:
  0.6 96.1 %shard_map.30 = (f32[2,512,256]{2,1,0:T(8,128)}, f32[2,512,256]{2,1,0:T(8,128)}, f32[16,2,8,8,128]{4,3,2,1,0:T(8,128)}) custom-call(f32[512,512]{1,0:T(8,128)} %x_ref.3), custom_call_target="tpu_custom_call" | custom-call | tf_op jit(solution)/shard_map/pallas_call | solution.py:247
  96.7 206.8 %shard_map.31 = (f32[512,512]{1,0:T(8,128)}, f32[512,512]{1,0:T(8,128)}) custom-call(f32[512,512]{1,0:T(8,128)} %x_ref.3, f32[2,512,256]{2,1,0:T(8,128)} %get-tuple-element.5.p_ref, f32[2,512,256]{2,1,0:T(8,128)} %get-tuple-element.6.cf, f32[16,2,8,8,128]{4,3,2,1,0:T(8,128)} %get-tuple-element.7.gall), custom_call_target="tpu_custom_call" | custom-call | tf_op jit(solution)/shard_map/pallas_call | solution.py:358

commit v3 on v2

--- a/solution.py
+++ b/solution.py
@@ -263,9 +263,16 @@
     )(matrix)
 
 
-def solve_kernel(stretch, x_ref, p_ref, cf, gall, upd, w_ref, g, m, t, e, bt, dcol, drow):
+def solve_kernel(stretch, x_hbm, p_hbm, cf_hbm, gall, upd, w_hbm, g, m, t, e, bt, dcol, drow, x_ref, p_ref, cf, w_ref, sems):
     n = 2 * PANEL
     col = lax.axis_index("col")
+    get_x = pltpu.make_async_copy(x_hbm, x_ref, sems.at[0])
+    get_p = pltpu.make_async_copy(p_hbm, p_ref, sems.at[1])
+    get_c = pltpu.make_async_copy(cf_hbm, cf, sems.at[2])
+    put_w = pltpu.make_async_copy(w_ref, w_hbm, sems.at[3])
+    get_c.start()
+    get_p.start()
+    get_x.start()
 
     @pl.loop(0, 16)
     def _(c):
@@ -339,10 +346,14 @@
         m[...] = t[...]
 
     m[...] = m[...] * drow[...]
+    get_c.wait()
     for k, h in enumerate(halves):
         c_top, c_low = cf[k, top, :], cf[k, low, :]
         w_ref[top, h] = dot(m[top, top], c_top)
         w_ref[low, h] = dot(m[low, top], c_top) + dot(m[low, low], c_low)
+    put_w.start()
+    get_p.wait()
+    get_x.wait()
     bt[:, top] = dott(p_ref[0], m[top, top])
     bt[:, low] = dott(p_ref[0], m[low, top]) + dott(p_ref[1], m[low, low])
     upd[:, low] = x_ref[:, low] - dot(bt[...], w_ref[:, low])
@@ -350,17 +361,22 @@
     first = jnp.where(col == 0, stretch * bt[:, top], first)
     first = first - dot(bt[:, low], w_ref[low, top])
     upd[:, top] = jnp.where(col == 1, stretch * bt[:, low], first)
+    put_w.wait()
 
 
 def solved(stretch, matrix, panels, cross, gram):
     vmem = pl.BlockSpec(memory_space=pltpu.VMEM)
+    anywhere = pl.BlockSpec(memory_space=pl.ANY)
     square = pltpu.VMEM((512, 512), F32)
     return pl.pallas_call(
         functools.partial(solve_kernel, stretch),
         out_shape=(jax.ShapeDtypeStruct((512, 512), F32), jax.ShapeDtypeStruct((512, 512), F32)),
-        in_specs=[vmem] * 4,
-        out_specs=(vmem, vmem),
-        scratch_shapes=[square] * 5 + [pltpu.VMEM((512, 1), F32), pltpu.VMEM((1, 512), F32)],
+        in_specs=[anywhere] * 3 + [vmem],
+        out_specs=(vmem, anywhere),
+        scratch_shapes=[square] * 5
+        + [pltpu.VMEM((512, 1), F32), pltpu.VMEM((1, 512), F32), square]
+        + [pltpu.VMEM((2, 512, PANEL), F32)] * 2
+        + [square, pltpu.SemaphoreType.DMA((4,))],
     )(matrix, panels, cross, gram)
 
 

time: 304 us -> 303 us (level)
  no operation moved by 1% of the time
where the time goes in v3:
time: 303 us
  Pallas kernels  302 us (100%)
    pallas_call x1, Pallas kernels, solved(): pl.pallas_call(functools.partial(solve_kernel, stretch), out_shape=(jax.S...  206 us
    pallas_call x1, Pallas kernels, reduced(): pl.pallas_call(reduce_kernel, out_shape=(out(2, 512, PANEL), out(2, 512,...  96.1 us

profile of v3, /device:TPU:1, one launch (start us, length us, event | category | flops | bytes accessed | tf_op | source)
XLA Modules:
  0.0 302.7 jit_solution(4141544525817535686)
XLA Ops:
  0.6 96.1 %shard_map.30 = (f32[2,512,256]{2,1,0:T(8,128)}, f32[2,512,256]{2,1,0:T(8,128)}, f32[16,2,8,8,128]{4,3,2,1,0:T(8,128)}) custom-call(f32[512,512]{1,0:T(8,128)} %x_hbm.1), custom_call_target="tpu_custom_call" | custom-call | tf_op jit(solution)/shard_map/pallas_call | solution.py:247
  96.7 205.9 %shard_map.31 = (f32[512,512]{1,0:T(8,128)}, f32[512,512]{1,0:T(8,128)}) custom-call(f32[512,512]{1,0:T(8,128)} %x_hbm.1, f32[2,512,256]{2,1,0:T(8,128)} %get-tuple-element.5.p_hbm, f32[2,512,256]{2,1,0:T(8,128)} %get-tuple-element.6.cf_hbm, f32[16,2,8,8,128]{4,3,2,1,0:T(8,128)} %get-tuple-element.7.gall), custom_call_target="tpu_custom_call" | custom-call | tf_op jit(solution)/shard_map/pallas_call | solution.py:371
